TPU v7x, 32 devices: a whole 2x2x4 slice. The times are simulated.
32 devices in a mesh: dp: 8 (over z, x), tensor: 4 (over y, core).
Axes of the slice: x: 2, y: 2, z: 4, core: 2. Of those that a mesh axis runs over, the one named last changes fastest.
Arguments:
- tokens: bfloat16 [16384, 768], P(('dp', 'tensor')), may hold values from -6 to 6
- context: bfloat16 [4096, 768], P(('dp', 'tensor')), may hold values from -6 to 6
- segment_ids: int32 [16384], P('dp'), may hold values from 0 to 3, as said below
- frame_ids: int32 [16384], P('dp'), may hold values from 0 to 63, as said below
- context_lengths: int32 [32], P('dp'), may hold values from 1 to 256, as said below
- cross_gain: float32 [768], replicated, may hold values from 0.25 to 1.75
- cross_bias: float32 [768], replicated, may hold values from -1.75 to 1.75
- cross_query: bfloat16 [768, 768], P(None, 'tensor'), may hold values from -0.21875 to 0.21875
- cross_key: bfloat16 [768, 768], P(None, 'tensor'), may hold values from -0.21875 to 0.21875
- cross_value: bfloat16 [768, 768], P(None, 'tensor'), may hold values from -0.21875 to 0.21875
- cross_out: bfloat16 [768, 768], P('tensor'), may hold values from -1.75 to 1.75
- attn_gain: float32 [768], replicated, may hold values from 0.25 to 1.75
- attn_bias: float32 [768], replicated, may hold values from -1.75 to 1.75
- attn_query: bfloat16 [768, 768], P(None, 'tensor'), may hold values from -0.21875 to 0.21875
- attn_key: bfloat16 [768, 768], P(None, 'tensor'), may hold values from -0.21875 to 0.21875
- attn_value: bfloat16 [768, 768], P(None, 'tensor'), may hold values from -0.21875 to 0.21875
- attn_out: bfloat16 [768, 768], P('tensor'), may hold values from -1.75 to 1.75
- mlp_gain: float32 [768], replicated, may hold values from 0.25 to 1.75
- mlp_bias: float32 [768], replicated, may hold values from -1.75 to 1.75
- mlp_up: bfloat16 [768, 3072], P(None, 'tensor'), may hold values from -0.21875 to 0.21875
- mlp_down: bfloat16 [3072, 768], P('tensor'), may hold values from -0.109375 to 0.109375
- out_grad: bfloat16 [16384, 768], P(('dp', 'tensor')), may hold values from -6 to 6
Outputs:
- block_out: bfloat16 [16384, 768], P(('dp', 'tensor'))
- tokens_grad: float32 [16384, 768], P(('dp', 'tensor'))
- context_grad: float32 [4096, 768], P(('dp', 'tensor'))
- cross_gain_grad: float32 [768], replicated
- cross_bias_grad: float32 [768], replicated
- cross_query_grad: float32 [768, 768], P(None, 'tensor')
- cross_key_grad: float32 [768, 768], P(None, 'tensor')
- cross_value_grad: float32 [768, 768], P(None, 'tensor')
- cross_out_grad: float32 [768, 768], P('tensor')
- attn_gain_grad: float32 [768], replicated
- attn_bias_grad: float32 [768], replicated
- attn_query_grad: float32 [768, 768], P(None, 'tensor')
- attn_key_grad: float32 [768, 768], P(None, 'tensor')
- attn_value_grad: float32 [768, 768], P(None, 'tensor')
- attn_out_grad: float32 [768, 768], P('tensor')
- mlp_gain_grad: float32 [768], replicated
- mlp_bias_grad: float32 [768], replicated
- mlp_up_grad: float32 [768, 3072], P(None, 'tensor')
- mlp_down_grad: float32 [3072, 768], P('tensor')
Inputs may be any that keep to these rules, and one draw needn't show every extreme that they name: `segment_ids`: within each aligned block of 2048 positions (one group) the ids never fall and take every value 0 to 3; every clip's token count is a multiple of its group's frame size, and each group has a clip of exactly 1024 tokens. `frame_ids`: groups alternate between frames of 64 tokens and frames of 16 tokens (which comes first is drawn); a token's frame id is its position within its clip divided by its group's frame size, rounded down. `context_lengths`: the 4 lengths of each group sum to 512, and each group has one of exactly 256; clip c's context features follow those of clips 0 to c - 1 in its group's block of context.
All inputs are finite; a program needn't handle non-finite values.
Results may differ from a plain program's by a relative error of at most 0.03.
Values may be sent and summed in bfloat16 or wider, within the bound.
No kernel may reach another device: no remote copies, remote signals or barrier semaphores. Data moves between devices by JAX's collectives and lax.ppermute only.
A program may use at most 128 MiB of HBM per device.

v0:
```python
import jax
import jax.numpy as jnp
from jax import lax
from jax.sharding import PartitionSpec as P

HEAD_DIM = 64


EPSILON = 1e-05


def layer_norm(inputs, norm_gain, norm_bias):
    average = jnp.mean(inputs, axis=-1, keepdims=True)
    centred = inputs - average
    variance = jnp.mean(centred * centred, axis=-1, keepdims=True)
    return centred * lax.rsqrt(variance + EPSILON) * norm_gain + norm_bias


def gelu_tanh(inputs):
    return jax.nn.gelu(inputs, approximate=True)


def contract_last(left, right):
    return lax.dot_general(
        left, right, (((1,), (1,)), ((), ())), preferred_element_type=jnp.float32
    )


def contract_first(left, right):
    return lax.dot_general(
        left, right, (((0,), (0,)), ((), ())), preferred_element_type=jnp.float32
    )


def project(normed, weight):
    gathered = lax.all_gather(normed, "tensor", axis=0, tiled=True)
    return (jnp.dot(gathered, weight, preferred_element_type=jnp.float32), gathered)


def weight_grad(kept, column_grads):
    return contract_first(kept, column_grads)


def spread_rows(mixed_rows, weight):
    return lax.psum_scatter(
        jnp.dot(mixed_rows, weight, preferred_element_type=jnp.float32).astype(jnp.bfloat16),
        "tensor",
        scatter_dimension=0,
        tiled=True,
    ).astype(jnp.float32)


def collect_rows(column_grads, weight):
    return lax.psum_scatter(
        contract_last(column_grads, weight).astype(jnp.bfloat16),
        "tensor",
        scatter_dimension=0,
        tiled=True,
    ).astype(jnp.float32)


def gather_grad(gradient):
    return lax.all_gather(gradient.astype(jnp.bfloat16), "tensor", axis=0, tiled=True)


def attend(queries, key_rows, value_rows, allowed_of, block_rows):
    block_count = queries.shape[0] // block_rows
    head_count = queries.shape[1] // HEAD_DIM
    score_scale = HEAD_DIM ** (-0.5)
    key_heads = key_rows.reshape(key_rows.shape[0], head_count, HEAD_DIM)
    value_heads = value_rows.reshape(value_rows.shape[0], head_count, HEAD_DIM)

    def one_block(block_index):
        query_heads = lax.dynamic_slice_in_dim(
            queries, block_index * block_rows, block_rows, 0
        ).reshape(block_rows, head_count, HEAD_DIM)
        scores = (
            jnp.einsum("qhd,khd->hqk", query_heads, key_heads, preferred_element_type=jnp.float32)
            * score_scale
        )
        scores = jnp.where(allowed_of(block_index)[None], scores, -1e30)
        row_max = jnp.max(scores, axis=-1, keepdims=True)
        exp_scores = jnp.exp(scores - row_max)
        row_total = jnp.sum(exp_scores, axis=-1, keepdims=True)
        weights_low = (exp_scores / row_total).astype(jnp.bfloat16)
        outputs = jnp.einsum(
            "hqk,khd->qhd", weights_low, value_heads, preferred_element_type=jnp.float32
        )
        return (
            outputs.reshape(block_rows, head_count * HEAD_DIM).astype(jnp.bfloat16),
            (row_max + jnp.log(row_total))[:, :, 0],
        )

    mixed_blocks, log_totals = lax.map(one_block, jnp.arange(block_count))
    return (mixed_blocks.reshape(queries.shape[0], -1), log_totals)


def attend_back(queries, key_rows, value_rows, log_totals, mixed_grad, allowed_of, block_rows):
    block_count = queries.shape[0] // block_rows
    head_count = queries.shape[1] // HEAD_DIM
    score_scale = HEAD_DIM ** (-0.5)
    key_heads = key_rows.reshape(key_rows.shape[0], head_count, HEAD_DIM)
    value_heads = value_rows.reshape(value_rows.shape[0], head_count, HEAD_DIM)

    def one_step(running, block_index):
        key_total, value_total = running
        query_heads = lax.dynamic_slice_in_dim(
            queries, block_index * block_rows, block_rows, 0
        ).reshape(block_rows, head_count, HEAD_DIM)
        grad_heads = lax.dynamic_slice_in_dim(
            mixed_grad, block_index * block_rows, block_rows, 0
        ).reshape(block_rows, head_count, HEAD_DIM)
        scores = (
            jnp.einsum("qhd,khd->hqk", query_heads, key_heads, preferred_element_type=jnp.float32)
            * score_scale
        )
        scores = jnp.where(allowed_of(block_index)[None], scores, -1e30)
        weights_full = jnp.exp(scores - log_totals[block_index][:, :, None])
        value_total = value_total + jnp.einsum(
            "hqk,qhd->khd",
            weights_full.astype(jnp.bfloat16),
            grad_heads,
            preferred_element_type=jnp.float32,
        )
        weight_grads = jnp.einsum(
            "qhd,khd->hqk", grad_heads, value_heads, preferred_element_type=jnp.float32
        )
        inner_sum = jnp.sum(weights_full * weight_grads, axis=-1, keepdims=True)
        score_grads = (weights_full * (weight_grads - inner_sum)).astype(jnp.bfloat16)
        query_grads = (
            jnp.einsum("hqk,khd->qhd", score_grads, key_heads, preferred_element_type=jnp.float32)
            * score_scale
        )
        key_total = (
            key_total
            + jnp.einsum(
                "hqk,qhd->khd", score_grads, query_heads, preferred_element_type=jnp.float32
            )
            * score_scale
        )
        return ((key_total, value_total), query_grads.reshape(block_rows, -1).astype(jnp.bfloat16))

    empty = jnp.zeros(key_heads.shape, jnp.float32)
    (key_total, value_total), query_blocks = lax.scan(
        one_step, (empty, empty), jnp.arange(block_count)
    )
    key_grads = key_total.reshape(key_rows.shape[0], -1).astype(jnp.bfloat16)
    value_grads = value_total.reshape(value_rows.shape[0], -1).astype(jnp.bfloat16)
    return (query_blocks.reshape(queries.shape[0], -1), key_grads, value_grads)


def shards(
    tokens,
    context,
    segment_ids,
    frame_ids,
    context_lengths,
    cross_gain,
    cross_bias,
    cross_query,
    cross_key,
    cross_value,
    cross_out,
    attn_gain,
    attn_bias,
    attn_query,
    attn_key,
    attn_value,
    attn_out,
    mlp_gain,
    mlp_bias,
    mlp_up,
    mlp_down,
    out_grad,
):
    group_rows = segment_ids.shape[0]
    block_rows = min(512, group_rows)
    context_rows = lax.all_gather(context, "tensor", axis=0, tiled=True)
    clip_ends = jnp.cumsum(context_lengths)
    context_ids = jnp.arange(context_rows.shape[0], dtype=jnp.int32)
    context_clip = jnp.sum((context_ids[:, None] >= clip_ends[None, :]).astype(jnp.int32), axis=1)

    def cross_allowed(block_index):
        own_segment = lax.dynamic_slice_in_dim(segment_ids, block_index * block_rows, block_rows, 0)
        return own_segment[:, None] == context_clip[None, :]

    def self_allowed(block_index):
        own_segment = lax.dynamic_slice_in_dim(segment_ids, block_index * block_rows, block_rows, 0)
        own_frame = lax.dynamic_slice_in_dim(frame_ids, block_index * block_rows, block_rows, 0)
        return (own_segment[:, None] == segment_ids[None, :]) & (
            frame_ids[None, :] <= own_frame[:, None]
        )

    start_rows = tokens.astype(jnp.float32)
    normed1, norm1_back = jax.vjp(layer_norm, start_rows, cross_gain, cross_bias)
    normed1 = normed1.astype(jnp.bfloat16)
    query1, kept1 = project(normed1, cross_query)
    query1 = query1.astype(jnp.bfloat16)
    cross_pair = jnp.concatenate([cross_key, cross_value], axis=1)
    width1 = cross_key.shape[1]
    keyval1 = jnp.dot(context_rows, cross_pair, preferred_element_type=jnp.float32).astype(
        jnp.bfloat16
    )
    key1 = keyval1[:, :width1]
    value1 = keyval1[:, width1:]
    mixed1, totals1 = attend(query1, key1, value1, cross_allowed, block_rows)
    hidden1 = start_rows + spread_rows(mixed1, cross_out)
    normed2, norm2_back = jax.vjp(layer_norm, hidden1, attn_gain, attn_bias)
    normed2 = normed2.astype(jnp.bfloat16)
    self_weight = jnp.concatenate([attn_query, attn_key, attn_value], axis=1)
    width2 = attn_query.shape[1]
    triple2, kept2 = project(normed2, self_weight)
    triple2 = triple2.astype(jnp.bfloat16)
    query2 = triple2[:, :width2]
    key2 = triple2[:, width2 : 2 * width2]
    value2 = triple2[:, 2 * width2 :]
    mixed2, totals2 = attend(query2, key2, value2, self_allowed, block_rows)
    hidden2 = hidden1 + spread_rows(mixed2, attn_out)
    normed3, norm3_back = jax.vjp(layer_norm, hidden2, mlp_gain, mlp_bias)
    normed3 = normed3.astype(jnp.bfloat16)
    upper_rows, kept3 = project(normed3, mlp_up)
    activated, gelu_back = jax.vjp(gelu_tanh, upper_rows)
    activated = activated.astype(jnp.bfloat16)
    final_rows = hidden2 + spread_rows(activated, mlp_down)
    block_out = final_rows.astype(jnp.bfloat16)
    grad3 = out_grad.astype(jnp.float32)
    grad3_rows = gather_grad(grad3)
    mlp_down_grad = contract_first(activated, grad3_rows)
    act_grad = contract_last(grad3_rows, mlp_down)
    upper_grad = gelu_back(act_grad)[0].astype(jnp.bfloat16)
    mlp_up_grad = weight_grad(kept3, upper_grad)
    normed3_grad = collect_rows(upper_grad, mlp_up)
    into3, mlp_gain_part, mlp_bias_part = norm3_back(normed3_grad)
    grad2 = grad3 + into3
    grad2_rows = gather_grad(grad2)
    attn_out_grad = contract_first(mixed2, grad2_rows)
    mixed2_grad = contract_last(grad2_rows, attn_out).astype(jnp.bfloat16)
    query2_grad, key2_grad, value2_grad = attend_back(
        query2, key2, value2, totals2, mixed2_grad, self_allowed, block_rows
    )
    triple2_grad = jnp.concatenate([query2_grad, key2_grad, value2_grad], axis=1)
    self_weight_grad = weight_grad(kept2, triple2_grad)
    attn_query_grad = self_weight_grad[:, :width2]
    attn_key_grad = self_weight_grad[:, width2 : 2 * width2]
    attn_value_grad = self_weight_grad[:, 2 * width2 :]
    normed2_grad = collect_rows(triple2_grad, self_weight)
    into2, attn_gain_part, attn_bias_part = norm2_back(normed2_grad)
    grad1 = grad2 + into2
    grad1_rows = gather_grad(grad1)
    cross_out_grad = contract_first(mixed1, grad1_rows)
    mixed1_grad = contract_last(grad1_rows, cross_out).astype(jnp.bfloat16)
    query1_grad, key1_grad, value1_grad = attend_back(
        query1, key1, value1, totals1, mixed1_grad, cross_allowed, block_rows
    )
    cross_query_grad = weight_grad(kept1, query1_grad)
    pair_grad = jnp.concatenate([key1_grad, value1_grad], axis=1)
    pair_weight_grad = contract_first(context_rows, pair_grad)
    cross_key_grad = pair_weight_grad[:, :width1]
    cross_value_grad = pair_weight_grad[:, width1:]
    normed1_part = contract_last(query1_grad, cross_query)
    context_part = contract_last(pair_grad, cross_pair)
    normed1_grad, context_grad = (
        lax.psum_scatter(
            normed1_part.astype(jnp.bfloat16), "tensor", scatter_dimension=0, tiled=True
        ).astype(jnp.float32),
        lax.psum_scatter(
            context_part.astype(jnp.bfloat16), "tensor", scatter_dimension=0, tiled=True
        ).astype(jnp.float32),
    )
    into1, cross_gain_part, cross_bias_part = norm1_back(normed1_grad)
    tokens_grad = grad1 + into1
    (
        cross_query_grad,
        cross_key_grad,
        cross_value_grad,
        cross_out_grad,
        attn_query_grad,
        attn_key_grad,
        attn_value_grad,
        attn_out_grad,
        mlp_up_grad,
        mlp_down_grad,
    ) = lax.psum(
        (
            cross_query_grad,
            cross_key_grad,
            cross_value_grad,
            cross_out_grad,
            attn_query_grad,
            attn_key_grad,
            attn_value_grad,
            attn_out_grad,
            mlp_up_grad,
            mlp_down_grad,
        ),
        "dp",
    )
    (
        cross_gain_grad,
        cross_bias_grad,
        attn_gain_grad,
        attn_bias_grad,
        mlp_gain_grad,
        mlp_bias_grad,
    ) = lax.psum(
        (
            cross_gain_part,
            cross_bias_part,
            attn_gain_part,
            attn_bias_part,
            mlp_gain_part,
            mlp_bias_part,
        ),
        ("dp", "tensor"),
    )
    return (
        block_out,
        tokens_grad,
        context_grad,
        cross_gain_grad,
        cross_bias_grad,
        cross_query_grad,
        cross_key_grad,
        cross_value_grad,
        cross_out_grad,
        attn_gain_grad,
        attn_bias_grad,
        attn_query_grad,
        attn_key_grad,
        attn_value_grad,
        attn_out_grad,
        mlp_gain_grad,
        mlp_bias_grad,
        mlp_up_grad,
        mlp_down_grad,
    )


def solution(mesh):
    in_specs = (
        P(("dp", "tensor"), None),
        P(("dp", "tensor"), None),
        P("dp"),
        P("dp"),
        P("dp"),
        P(),
        P(),
        P(None, "tensor"),
        P(None, "tensor"),
        P(None, "tensor"),
        P("tensor", None),
        P(),
        P(),
        P(None, "tensor"),
        P(None, "tensor"),
        P(None, "tensor"),
        P("tensor", None),
        P(),
        P(),
        P(None, "tensor"),
        P("tensor", None),
        P(("dp", "tensor"), None),
    )
    out_specs = (
        P(("dp", "tensor"), None),
        P(("dp", "tensor"), None),
        P(("dp", "tensor"), None),
        P(),
        P(),
        P(None, "tensor"),
        P(None, "tensor"),
        P(None, "tensor"),
        P("tensor", None),
        P(),
        P(),
        P(None, "tensor"),
        P(None, "tensor"),
        P(None, "tensor"),
        P("tensor", None),
        P(),
        P(),
        P(None, "tensor"),
        P("tensor", None),
    )
    return jax.shard_map(shards, mesh=mesh, in_specs=in_specs, out_specs=out_specs, check_vma=False)
```

profile of v0, /device:TPU:0, one launch (start us, length us, event | category | flops | bytes accessed | tf_op | source)
XLA Modules:
  0.0 1156.1 jit_solution(14333139804636595822)
XLA Ops:
  14.2 10.1 all_gather.22
  25.8 19.4 %all-gather.7.cloned.1.call-done = bf16[2048,768]{1,0:T(8,128)(2,1)} async-done(((bf16[512,768]{1,0:T(8,128)(2,1)}), bf16[2048,768]{1,0:T(8,128)(2,1)}) %all-gather.7.cloned.1.call-update) | async-done | bytes 3145744 | tf_op jit(solution)/shard_map/all_gather | solution.py:36
  48.4 16.7 %while.54 = (s32[]{:T(128)}, bf16[4,512,192]{1,2,0:T(8,128)(2,1)S(1)}, f32[4,3,512]{2,1,0:T(4,128)S(1)}, s32[4]{0:T(128)S(1)}, s32[2048]{0:T(1024)S(1)}, /*index...) while((s32[]{:T(128)}, ...), condition=%wide.region_7.8_spmd, body=%wide.region_4.7_spmd.sunk | while | flops 211122688 | bytes 12122319 | solution.py:94
  69.2 38.0 %reduce-scatter.8.cloned.1.call-done = bf16[512,768]{1,0:T(8,128)(2,1)} async-done(((bf16[2048,768]{1,0:T(8,128)(2,1)}), bf16[512,768]{1,0:T(8,128)(2,1)}) %reduce-scatter.8.cloned.1.call-update) | async-done | bytes 786448 | tf_op jit(solution)/shard_map/reduce_scatter | solution.py:45
  115.1 25.3 %all-gather.9.cloned.1.call-done = bf16[2048,768]{1,0:T(8,128)(2,1)} async-done(((bf16[512,768]{1,0:T(8,128)(2,1)}), bf16[2048,768]{1,0:T(8,128)(2,1)}) %all-gather.9.cloned.1.call-update) | async-done | bytes 3145744 | tf_op jit(solution)/shard_map/all_gather | solution.py:36
  147.9 99.3 %while.55 = (s32[]{:T(128)}, bf16[4,512,192]{1,2,0:T(8,128)(2,1)}, f32[4,3,512]{2,1,0:T(4,128)}, s32[4]{0:T(128)}, s32[2048]{0:T(1024)S(1)}, /*index=5*/s32[2048...) while((s32[]{:T(128)}, bf16[4,512,192]{1,2,0:T(8,128)(2,1)}, ...), condition=%wide.region_14.15_spmd, body=%wide.region_11.14_spmd.sunk | while | flops 846297600 | bytes 44775632 | solution.py:94
  253.7 37.5 %reduce-scatter.10.cloned.1.call-done = bf16[512,768]{1,0:T(8,128)(2,1)} async-done(((bf16[2048,768]{1,0:T(8,128)(2,1)}), bf16[512,768]{1,0:T(8,128)(2,1)}) %reduce-scatter.10.cloned.1.call-update) | async-done | bytes 786448 | tf_op jit(solution)/shard_map/reduce_scatter | solution.py:45
  295.5 25.6 %all-gather.13.cloned.1.call-done = bf16[2048,768]{1,0:T(8,128)(2,1)} async-done(((bf16[512,768]{1,0:T(8,128)(2,1)}), bf16[2048,768]{1,0:T(8,128)(2,1)}) %all-gather.13.cloned.1.call-update) | async-done | bytes 3145744 | tf_op jit(solution)/shard_map/all_gather | solution.py:63
  321.1 7.6 fusion.88
  328.7 23.0 %all-gather.11.cloned.1.call-done = bf16[2048,768]{1,0:T(8,128)(2,1)} async-done(((bf16[512,768]{1,0:T(8,128)(2,1)}), bf16[2048,768]{1,0:T(8,128)(2,1)}) %all-gather.11.cloned.1.call-update) | async-done | bytes 3145744 | tf_op jit(solution)/shard_map/all_gather | solution.py:36
  351.7 11.8 %fusion.44 = (bf16[2048,768]{1,0:T(8,128)(2,1)S(1)}, f32[2048,768]{1,0:T(8,128)}) fusion(f32[2048,768]{1,0:T(8,128)} %fusion.88, bf16[2048,768]{1,0:T(8,128)(2,1)} %all-gather.11.cloned.1.call-done, bf16[768,768]{1,0:T(8,128)(2,1)S(1)} %copy-done), kind=kOutput, calls=%fused_computation.71 | convolution fusion | flops 2447376384 | bytes 20054016 | tf_op jit(solution)/shard_map/dot_general | solution.py:37
  370.4 8.3 convolution_convert_fusion.1
  378.7 28.5 %reduce-scatter.14.cloned.1.call-done = bf16[512,768]{1,0:T(8,128)(2,1)} async-done(((bf16[2048,768]{1,0:T(8,128)(2,1)}), bf16[512,768]{1,0:T(8,128)(2,1)}) %reduce-scatter.14.cloned.1.call-update) | async-done | bytes 786448 | tf_op jit(solution)/shard_map/reduce_scatter | solution.py:54
  409.6 38.3 %reduce-scatter.12.cloned.1.call-done = bf16[512,768]{1,0:T(8,128)(2,1)} async-done(((bf16[2048,768]{1,0:T(8,128)(2,1)}), bf16[512,768]{1,0:T(8,128)(2,1)}) %reduce-scatter.12.cloned.1.call-update) | async-done | bytes 786448 | tf_op jit(solution)/shard_map/reduce_scatter | solution.py:45
  453.2 28.6 %all-gather.15.cloned.1.call-done = bf16[2048,768]{1,0:T(8,128)(2,1)} async-done(((bf16[512,768]{1,0:T(8,128)(2,1)}), bf16[2048,768]{1,0:T(8,128)(2,1)}) %all-gather.15.cloned.1.call-update) | async-done | bytes 3145744 | tf_op jit(solution)/shard_map/all_gather | solution.py:63
  485.9 140.2 %while.56 = (s32[]{:T(128)}, f32[2048,3,64]{0,2,1:T(8,128)}, f32[2048,3,64]{0,2,1:T(8,128)}, bf16[4,512,192]{1,2,0:T(8,128)(2,1)}, s32[4]{0:T(128)S(1)}, /*index...) while((s32[]{:T(128)}, f32[2048,3,64]{0,2,1:T(8,128)}, ...), condition=%wide.region_24.25_spmd.clone, body=%wide.region_22.24_spmd.clone.sunk | while | flops 2065758720 | bytes 151394768 | solution.py:144
  637.2 38.0 %reduce-scatter.16.cloned.1.call-done = bf16[512,768]{1,0:T(8,128)(2,1)} async-done(((bf16[2048,768]{1,0:T(8,128)(2,1)}), bf16[512,768]{1,0:T(8,128)(2,1)}) %reduce-scatter.16.cloned.1.call-update) | async-done | bytes 786448 | tf_op jit(solution)/shard_map/reduce_scatter | solution.py:54
  682.3 28.6 %all-gather.17.cloned.1.call-done = bf16[2048,768]{1,0:T(8,128)(2,1)} async-done(((bf16[512,768]{1,0:T(8,128)(2,1)}), bf16[2048,768]{1,0:T(8,128)(2,1)}) %all-gather.17.cloned.1.call-update) | async-done | bytes 3145744 | tf_op jit(solution)/shard_map/all_gather | solution.py:63
  714.6 40.6 %while.57 = (s32[]{:T(128)}, f32[512,3,64]{0,2,1:T(8,128)S(1)}, f32[512,3,64]{0,2,1:T(8,128)S(1)}, bf16[4,512,192]{1,2,0:T(8,128)(2,1)S(1)}, s32[4]{0:T(128)}, /...) while((s32[]{:T(128)}, f32[512,3,64]{0,2,1:T(8,128)S(1)}, ...), condition=%wide.region_30.31_spmd.clone, body=%wide.region_28.30_spmd.clone.sunk | while | flops 511343104 | bytes 28481816 | solution.py:144
  761.0 7.2 fusion.91
  768.2 7.6 fusion.78
  788.7 33.1 %reduce-scatter.18.cloned.1.call-done = bf16[512,768]{1,0:T(8,128)(2,1)} async-done(((bf16[2048,768]{1,0:T(8,128)(2,1)}), bf16[512,768]{1,0:T(8,128)(2,1)}) %reduce-scatter.18.cloned.1.call-update) | async-done | bytes 786448 | tf_op jit(solution)/shard_map/reduce_scatter | solution.py:263
  825.7 43.7 %all-reduce = (f32[768]{0:T(1024)}, f32[768]{0:T(1024)}, f32[768]{0:T(1024)}, f32[768]{0:T(1024)}, f32[768]{0:T(1024)}, /*index=5*/f32[768]{0:T(1024)}) all-reduce(f32[768]{0:T(1024)S(1)} %get-tuple-element.335, f32[768]{0:T(1024)S(1)} %get-tuple-element.340, ...), channel_id=1, replica_groups=mesh['dp'=8,'tensor'=4] {'dp','tensor'}, use_global_device_ids=true, to_apply=%region_36.37 | all-reduce | flops 4608 | bytes 36864 | tf_op jit(solution)/shard_map/psum | solution.py:305
  871.2 265.3 %all-reduce.4.cloned.1.call-done = (f32[768,192]{0,1:T(8,128)}, f32[768,192]{0,1:T(8,128)}, f32[768,192]{0,1:T(8,128)}, f32[192,768]{1,0:T(8,128)}, f32[768,192]...) async-done(((f32[768,192]{0,1:T(8,128)}, f32[768,192]{0,1:T(8,128)}, ...) | async-done | bytes 9437200 | tf_op jit(solution)/shard_map/psum | solution.py:283
  (515 shorter events, 388.1 us)
Async XLA Ops:
  7.2 344.5 %copy-start = (bf16[768,768]{1,0:T(8,128)(2,1)S(1)}, bf16[768,768]{1,0:T(8,128)(2,1)}, u32[]{:S(2)}) copy-start(bf16[768,768]{1,0:T(8,128)(2,1)} %param.49) | copy-start | bytes 3538948
  7.2 38.0 %all-gather.7.cloned.1.call-start = ((), (), s32[]{:S(2)}) async-start(), calls=%async_computation.7 | async-start | bytes 3932160 | tf_op jit(solution)/shard_map/all_gather | solution.py:36
  13.8 93.4 %reduce-scatter.8.cloned.1.call-start = ((), (), s32[]{:S(2)}) async-start(), calls=%async_computation.8 | async-start | bytes 3932160 | tf_op jit(solution)/shard_map/reduce_scatter | solution.py:45
  69.1 41.2 %copy-start.67 = (f32[768]{0:T(1024)S(1)}, f32[768]{0:T(1024)}, u32[]{:S(2)}) copy-start(f32[768]{0:T(1024)} %param.41) | copy-start | bytes 9220
  69.1 41.2 %copy-start.85 = (f32[768]{0:T(1024)S(1)}, f32[768]{0:T(1024)}, u32[]{:S(2)}) copy-start(f32[768]{0:T(1024)} %param.42) | copy-start | bytes 9220
  69.1 42.8 %copy-start.52 = (bf16[768,192]{0,1:T(8,128)(2,1)S(1)}, bf16[768,192]{0,1:T(8,128)(2,1)}, u32[]{:S(2)}) copy-start(bf16[768,192]{0,1:T(8,128)(2,1)} %param.43) | copy-start | bytes 884740
  69.1 43.5 %copy-start.53 = (bf16[768,192]{0,1:T(8,128)(2,1)S(1)}, bf16[768,192]{0,1:T(8,128)(2,1)}, u32[]{:S(2)}) copy-start(bf16[768,192]{0,1:T(8,128)(2,1)} %param.44) | copy-start | bytes 884740
  69.1 71.2 %all-gather.9.cloned.1.call-start = ((), (), s32[]{:S(2)}) async-start(), calls=%async_computation.9 | async-start | bytes 3932160 | tf_op jit(solution)/shard_map/all_gather | solution.py:36
  111.6 179.5 %reduce-scatter.10.cloned.1.call-start = ((), (), s32[]{:S(2)}) async-start(), calls=%async_computation.10 | async-start | bytes 3932160 | tf_op jit(solution)/shard_map/reduce_scatter | solution.py:45
  253.0 68.1 %all-gather.13.cloned.1.call-start = ((), (), s32[]{:S(2)}) async-start(), calls=%async_computation.13 | async-start | bytes 3932160 | tf_op jit(solution)/shard_map/all_gather | solution.py:63
  253.6 98.0 %all-gather.11.cloned.1.call-start = ((), (), s32[]{:S(2)}) async-start(), calls=%async_computation.11 | async-start | bytes 3932160 | tf_op jit(solution)/shard_map/all_gather | solution.py:36
  295.1 112.2 %reduce-scatter.14.cloned.1.call-start = ((), (), s32[]{:S(2)}) async-start(), calls=%async_computation.14 | async-start | bytes 3932160 | tf_op jit(solution)/shard_map/reduce_scatter | solution.py:54
  369.1 78.8 %reduce-scatter.12.cloned.1.call-start = ((), (), s32[]{:S(2)}) async-start(), calls=%async_computation.12 | async-start | bytes 3932160 | tf_op jit(solution)/shard_map/reduce_scatter | solution.py:45
  378.7 103.2 %all-gather.15.cloned.1.call-start = ((), (), s32[]{:S(2)}) async-start(), calls=%async_computation.15 | async-start | bytes 3932160 | tf_op jit(solution)/shard_map/all_gather | solution.py:63
  409.6 42.4 %copy-start.23 = (bf16[512,768]{1,0:T(8,128)(2,1)S(1)}, bf16[512,768]{1,0:T(8,128)(2,1)}, u32[]{:S(2)}) copy-start(bf16[512,768]{1,0:T(8,128)(2,1)} %param.51) | copy-start | bytes 2359300
  453.2 222.1 %reduce-scatter.16.cloned.1.call-start = ((), (), s32[]{:S(2)}) async-start(), calls=%async_computation.16 | async-start | bytes 3932160 | tf_op jit(solution)/shard_map/reduce_scatter | solution.py:54
  637.1 42.8 %copy-start.15 = (f32[512,768]{1,0:T(8,128)S(1)}, f32[512,768]{1,0:T(8,128)}, u32[]{:S(2)}) copy-start(f32[512,768]{1,0:T(8,128)} %copy-done.14) | copy-start | bytes 4718596
  637.1 42.8 %copy-start.81 = (f32[512]{0:T(512)S(1)}, f32[512]{0:T(512)}, u32[]{:S(2)}) copy-start(f32[512]{0:T(512)} %copy-done.80) | copy-start | bytes 6148
  637.2 73.8 %all-gather.17.cloned.1.call-start = ((), (), s32[]{:S(2)}) async-start(), calls=%async_computation.17 | async-start | bytes 3932160 | tf_op jit(solution)/shard_map/all_gather | solution.py:63
  682.2 104.7 %reduce-scatter.20.cloned.1.call-start = ((), (), s32[]{:S(2)}) async-start(), calls=%async_computation.19 | async-start | bytes 983040 | tf_op jit(solution)/shard_map/reduce_scatter | solution.py:266
  757.9 63.9 %reduce-scatter.18.cloned.1.call-start = ((), (), s32[]{:S(2)}) async-start(), calls=%async_computation.18 | async-start | bytes 3932160 | tf_op jit(solution)/shard_map/reduce_scatter | solution.py:263
  760.7 375.8 %all-reduce.4.cloned.1.call-start = ((), (), s32[]{:S(2)}) async-start(), calls=%async_computation.20 | async-start | bytes 18874368 | tf_op jit(solution)/shard_map/psum | solution.py:283
  786.9 82.6 %copy-start.26 = (f32[512,768]{1,0:T(8,128)S(1)}, f32[512,768]{1,0:T(8,128)}, u32[]{:S(2)}) copy-start(f32[512,768]{1,0:T(8,128)} %get-tuple-element.443) | copy-start | bytes 4718596
  821.8 47.6 %copy-start.22 = (bf16[512,768]{1,0:T(8,128)(2,1)S(1)}, bf16[512,768]{1,0:T(8,128)(2,1)}, u32[]{:S(2)}) copy-start(bf16[512,768]{1,0:T(8,128)(2,1)} %reduce-scatter.18.cloned.1.call-done) | copy-start | bytes 2359300
  (100 other events, 1221.2 us)
Sparse Core Ops, SparseCore 0:
  13.9 31.2 all-gather.6
  69.2 37.9 reduce-scatter.7
  111.8 28.5 all-gather.8
  253.2 37.9 reduce-scatter.9
  292.5 28.5 all-gather.12
  323.1 28.5 all-gather.10
  369.2 37.9 reduce-scatter.13
  409.9 37.9 reduce-scatter.11
  453.3 28.5 all-gather.14
  637.3 37.9 reduce-scatter.15
  682.4 28.5 all-gather.16
  758.0 23.2 reduce-scatter.19
  783.8 37.9 reduce-scatter.17
  830.7 305.7 all-reduce.3
where the time goes:
time: 1160 us
  waiting for transfers between devices  630 us (54%)
  matrix products  245 us (21%)
  other arithmetic  106 us (9%)
  local copies, waits for them, and re-layouts  77.1 us (7%)
  blocking collectives  53.8 us (5%)
  loops' own time  27.5 us (2%)
  between operations  15.1 us (1%)
    psum x1, waiting for transfers between devices, shards(): lax.psum((cross_query_grad, cross_key_grad, cross_value_grad, cross_out_g...  265 us
    reduce_scatter x3, waiting for transfers between devices, spread_rows(): lax.psum_scatter(jnp.dot(mixed_rows, weight, preferred_element_type=jnp.f...  114 us
    all_gather x3, waiting for transfers between devices, gather_grad(): lax.all_gather(gradient.astype(jnp.bfloat16), 'tensor', axis=0, tiled=True)  82.8 us
    all_gather x3, waiting for transfers between devices, project(): gathered = lax.all_gather(normed, 'tensor', axis=0, tiled=True)  67.7 us
    reduce_scatter x2, waiting for transfers between devices, collect_rows(): lax.psum_scatter(contract_last(column_grads, weight).astype(jnp.bfloat16)...  66.5 us
    psum x1, blocking collectives, shards(): lax.psum((cross_gain_part, cross_bias_part, attn_gain_part, attn_bias_par...  43.7 us
    reduce_scatter x1, waiting for transfers between devices, shards(): lax.psum_scatter(normed1_part.astype(jnp.bfloat16), 'tensor', scatter_dim...  33.1 us
    dot_general x8, matrix products, one_block(): jnp.einsum('hqk,khd->qhd', weights_low, value_heads, preferred_element_ty...  31.6 us
  transfers between devices with their start and end apart: 14, of which 13 were waited for; matrix products, arithmetic and copies ran while one was open for 5% of the time, Pallas kernels for 0%

commit v1 on v0

v1 whole, which is shorter than its diff:
```python
import functools

import jax
import jax.numpy as jnp
from jax import lax
from jax.experimental import pallas as pl
from jax.experimental.pallas import tpu as pltpu
from jax.sharding import PartitionSpec as P

HEAD_DIM = 64
EPSILON = 1e-05
BLOCK = 256
WIDE = 256
FAR = -(2.0**100)
LOW = jnp.bfloat16
F32 = jnp.float32


def dot(left, right, left_dim, right_dim):
    return lax.dot_general(
        left, right, (((left_dim,), (right_dim,)), ((), ())), preferred_element_type=F32
    )


def swap(values, axis, bit):
    size = lax.axis_size(axis)
    return lax.ppermute(values, axis, [(i, i ^ bit) for i in range(size)])


def gather_pieces(own):
    near = swap(own, "tensor", 1)
    far = swap(own, "tensor", 2)
    return [own, near, far, swap(far, "tensor", 1)]


def reduce_pieces(pieces):
    pieces = lax.optimization_barrier(tuple(piece.astype(LOW) for piece in pieces))
    near_own = swap(pieces[1], "tensor", 1)
    near_far = swap(pieces[3], "tensor", 1)
    far = (pieces[2].astype(F32) + near_far.astype(F32)).astype(LOW)
    from_far = swap(far, "tensor", 2)
    return pieces[0].astype(F32) + near_own.astype(F32) + from_far.astype(F32)


def trade_pieces(pieces):
    return [pieces[0]] + [swap(pieces[r], "tensor", r) for r in range(1, 4)]


def sum_over_groups(values, turn):
    size = lax.axis_size("dp")
    place = lax.axis_index("dp")
    bits = [1 << b for b in range(size.bit_length() - 1)]
    bits = bits[turn:] + bits[:turn]
    values = values.astype(LOW)
    for bit in bits:
        half = values.shape[0] // 2
        side = (place // bit) % 2
        keep = lax.dynamic_slice_in_dim(values, side * half, half, 0)
        send = lax.dynamic_slice_in_dim(values, (1 - side) * half, half, 0)
        received = swap(send, "dp", bit)
        values = (keep.astype(F32) + received.astype(F32)).astype(LOW)
    for bit in reversed(bits):
        side = (place // bit) % 2
        received = swap(values, "dp", bit)
        values = jnp.where(
            side == 1,
            jnp.concatenate([received, values], 0),
            jnp.concatenate([values, received], 0),
        )
    return values.astype(F32)


def sum_everywhere(values):
    for axis in ("tensor", "dp"):
        size = lax.axis_size(axis)
        for b in range(size.bit_length() - 1):
            values = values + swap(values, axis, 1 << b)
    return values


def place_of(index, turn, per):
    return ((index // per) ^ turn) * per + index % per


def with_marks(values, marks):
    return jnp.concatenate([values[:, :128], values[:, 128:] + marks], axis=1)


def head_mask(shape, head, heads, keep_marks):
    lane = lax.broadcasted_iota(jnp.int32, shape, len(shape) - 1)
    own = lane // HEAD_DIM == head
    if keep_marks:
        own = own | (lane >= heads * HEAD_DIM)
    return own


def attend_kernel(
    plan, q_ref, k_ref, v_ref, qmark_ref, kmark_ref, *rest, heads, causal, blocks, per
):
    if causal:
        qframe_ref, kframe_ref, out_ref, stat_ref, top_s, acc_s = rest
    else:
        out_ref, stat_ref, top_s, acc_s = rest
    index = pl.program_id(1)
    turn = plan[0]
    marked = with_marks(q_ref[...] * LOW(HEAD_DIM**-0.5), qmark_ref[...])
    queries = [
        jnp.where(head_mask((BLOCK, WIDE), h, heads, True), marked, LOW(0)) for h in range(heads)
    ]
    lane = lax.broadcasted_iota(jnp.int32, (BLOCK, WIDE), 1)
    top_s[...] = jnp.full_like(top_s, -3.0e38)
    acc_s[...] = jnp.zeros_like(acc_s)

    def step(j, diagonal):
        row = pl.multiple_of(place_of(j, turn, per) * BLOCK, BLOCK)
        keys = with_marks(
            k_ref[pl.ds(row, BLOCK), :],
            kmark_ref[pl.ds(pl.multiple_of(j * BLOCK, BLOCK), BLOCK), :],
        )
        values = jnp.where(lane == heads * HEAD_DIM, LOW(1), v_ref[pl.ds(row, BLOCK), :])
        for h in range(heads):
            scores = dot(queries[h], keys, 1, 1)
            if diagonal:
                scores = jnp.where(kframe_ref[...] <= qframe_ref[...], scores, FAR)
            before = top_s[h]
            top = jnp.maximum(before, jnp.max(scores, axis=1, keepdims=True))
            weights = jnp.exp(scores - top[:, :1]).astype(LOW)
            shrink = jnp.exp(before - top)
            top_s[h] = top
            acc_s[h] = acc_s[h] * shrink[:, :1] + dot(weights, values, 1, 0)

    low = plan[1 + index]
    high = index if causal else plan[1 + blocks + index]

    def body(j, carry):
        step(j, False)
        return carry

    lax.fori_loop(low, high, body, 0)
    if causal:
        step(index, True)
    out = jnp.zeros((BLOCK, WIDE), F32)
    stats = jnp.zeros((BLOCK, 128), F32)
    for h in range(heads):
        total = acc_s[h][:, heads * HEAD_DIM : heads * HEAD_DIM + 1]
        out = jnp.where(head_mask((BLOCK, WIDE), h, heads, False), acc_s[h] / total, out)
        stats = jnp.where(
            lax.broadcasted_iota(jnp.int32, (BLOCK, 128), 1) == h,
            top_s[h] + jnp.log(total),
            stats,
        )
    out_ref[...] = out[:, : out_ref.shape[1]].astype(LOW)
    stat_ref[...] = stats.T[:8]


def attend(plan, qkv, lanes, marks, frames, out_cols, heads, repeat, per):
    q, k, v = qkv
    rows, keys = q.shape[0], k.shape[0]
    blocks = rows // BLOCK
    causal = frames is not None
    qmarks, kmarks = marks

    def turned(i, plan):
        return place_of(i, plan[0], per)

    in_specs = [
        pl.BlockSpec((BLOCK, WIDE), lambda r, i, plan: (turned(i, plan), lanes[0] + r)),
        pl.BlockSpec((keys, WIDE), lambda r, i, plan: (0, lanes[1] + r)),
        pl.BlockSpec((keys, WIDE), lambda r, i, plan: (0, lanes[2] + r)),
        pl.BlockSpec((BLOCK, 128), lambda r, i, plan: (i, 0)),
        pl.BlockSpec((keys, 128), lambda r, i, plan: (0, 0)),
    ]
    operands = [q, k, v, qmarks, kmarks]
    if causal:
        in_specs += [
            pl.BlockSpec((BLOCK, 1), lambda r, i, plan: (i, 0)),
            pl.BlockSpec((1, BLOCK), lambda r, i, plan: (0, i)),
        ]
        operands += [frames[:, None], frames[None, :]]
    area = rows * keys * heads * repeat // (3 if causal else 1)
    return pl.pallas_call(
        functools.partial(attend_kernel, heads=heads, causal=causal, blocks=blocks, per=per),
        grid_spec=pltpu.PrefetchScalarGridSpec(
            num_scalar_prefetch=1,
            grid=(repeat, blocks),
            in_specs=in_specs,
            out_specs=[
                pl.BlockSpec((BLOCK, out_cols), lambda r, i, plan: (turned(i, plan), r)),
                pl.BlockSpec((8, BLOCK), lambda r, i, plan: (r, i)),
            ],
            scratch_shapes=[
                pltpu.VMEM((heads, BLOCK, 128), F32),
                pltpu.VMEM((heads, BLOCK, WIDE), F32),
            ],
        ),
        out_shape=[
            jax.ShapeDtypeStruct((rows, out_cols * repeat), LOW),
            jax.ShapeDtypeStruct((8 * repeat, rows), F32),
        ],
        cost_estimate=pl.CostEstimate(
            flops=area * HEAD_DIM * 16, bytes_accessed=rows * 3000, transcendentals=area
        ),
        name="attend_self" if causal else "attend_cross",
    )(plan, *operands)


def attend_back_kernel(
    plan,
    q_ref,
    k_ref,
    v_ref,
    grad_ref,
    out_ref,
    stat_ref,
    qmark_ref,
    kmark_ref,
    *rest,
    heads,
    causal,
    blocks,
    key_blocks,
    per,
):
    if causal:
        qframe_ref, kframe_ref, *rest = rest
    dq_ref, dk_ref, dv_ref, q_s, g_s, inner_s, dq_s, dk_s, dv_s = rest
    j = pl.program_id(1)
    turn = plan[0]
    cols = heads * HEAD_DIM

    @pl.when(j == 0)
    def _():
        dq_s[...] = jnp.zeros_like(dq_s)

        def prepare(i, carry):
            spot = pl.ds(pl.multiple_of(i * BLOCK, BLOCK), BLOCK)
            row = pl.ds(pl.multiple_of(place_of(i, turn, per) * BLOCK, BLOCK), BLOCK)
            marked = with_marks(q_ref[row, :] * LOW(HEAD_DIM**-0.5), qmark_ref[spot, :])
            grads = grad_ref[row, :]
            product = grads[:, :cols].astype(F32) * out_ref[row, :][:, :cols].astype(F32)
            upper = product.astype(LOW)
            lower = (product - upper.astype(F32)).astype(LOW)
            lane = lax.broadcasted_iota(jnp.int32, (8, cols), 1)
            pick = (
                lane // HEAD_DIM == lax.broadcasted_iota(jnp.int32, (8, cols), 0)
            ).astype(LOW)
            inner_s[:, spot] = dot(pick, upper, 1, 1) + dot(pick, lower, 1, 1)
            for h in range(heads):
                mask = head_mask((BLOCK, WIDE), h, heads, True)
                q_s[h, spot, :] = jnp.where(mask, marked, LOW(0))
                g_s[h, spot, :] = jnp.where(
                    head_mask((BLOCK, WIDE), h, heads, False), grads, LOW(0)
                )
            return carry

        lax.fori_loop(0, blocks, prepare, 0)

    keys = k_ref[...]
    keys_turned = keys.astype(F32).T.astype(LOW)
    keys = with_marks(keys, kmark_ref[...])
    values = v_ref[...]
    dk_s[...] = jnp.zeros_like(dk_s)
    dv_s[...] = jnp.zeros_like(dv_s)

    def step(i, diagonal):
        spot = pl.ds(pl.multiple_of(i * BLOCK, BLOCK), BLOCK)
        for h in range(heads):
            queries = q_s[h, spot, :]
            grads = g_s[h, spot, :]
            scores = dot(keys, queries, 1, 1)
            if diagonal:
                scores = jnp.where(kframe_ref[...] <= qframe_ref[...], scores, FAR)
            weights = jnp.exp(scores - stat_ref[h : h + 1, spot])
            weight_grads = dot(values, grads, 1, 1)
            score_grads = (weights * (weight_grads - inner_s[h : h + 1, spot])).astype(LOW)
            dv_s[...] += dot(weights.astype(LOW), grads, 1, 0)
            dk_s[...] += dot(score_grads, queries, 1, 0)
            part = slice(h * HEAD_DIM, (h + 1) * HEAD_DIM)
            dq_s[part, spot] += dot(keys_turned[part], score_grads, 1, 0)

    low = j + 1 if causal else plan[1 + 2 * blocks + j]
    high = plan[1 + 2 * blocks + key_blocks + j]
    if causal:
        step(j, True)

    def body(i, carry):
        step(i, False)
        return carry

    lax.fori_loop(low, high, body, 0)
    dk_ref[...] = dk_s[...].astype(LOW)
    dv_ref[...] = dv_s[...].astype(LOW)

    @pl.when(j == key_blocks - 1)
    def _():
        def finish(i, carry):
            spot = pl.ds(pl.multiple_of(i * BLOCK, BLOCK), BLOCK)
            row = pl.ds(pl.multiple_of(place_of(i, turn, per) * BLOCK, BLOCK), BLOCK)
            dq_ref[row, :] = (dq_s[:, spot].T * HEAD_DIM**-0.5).astype(LOW)
            return carry

        lax.fori_loop(0, blocks, finish, 0)


def attend_back(plan, qkv, lanes, grads, out, out_cols, stats, marks, frames, heads, repeat, per):
    q, k, v = qkv
    rows, keys = q.shape[0], k.shape[0]
    blocks, key_blocks = rows // BLOCK, keys // BLOCK
    causal = frames is not None
    qmarks, kmarks = marks

    def turned(i, plan):
        return place_of(i, plan[0], per)

    in_specs = [
        pl.BlockSpec((rows, WIDE), lambda r, j, plan: (0, lanes[0] + r)),
        pl.BlockSpec((BLOCK, WIDE), lambda r, j, plan: (turned(j, plan), lanes[1] + r)),
        pl.BlockSpec((BLOCK, WIDE), lambda r, j, plan: (turned(j, plan), lanes[2] + r)),
        pl.BlockSpec((rows, WIDE), lambda r, j, plan: (0, r)),
        pl.BlockSpec((rows, out_cols), lambda r, j, plan: (0, r)),
        pl.BlockSpec((8, rows), lambda r, j, plan: (r, 0)),
        pl.BlockSpec((rows, 128), lambda r, j, plan: (0, 0)),
        pl.BlockSpec((BLOCK, 128), lambda r, j, plan: (j, 0)),
    ]
    operands = [q, k, v, grads, out, stats, qmarks, kmarks]
    if causal:
        in_specs += [
            pl.BlockSpec((1, BLOCK), lambda r, j, plan: (0, j)),
            pl.BlockSpec((BLOCK, 1), lambda r, j, plan: (j, 0)),
        ]
        operands += [frames[None, :], frames[:, None]]
    area = rows * keys * heads * repeat // (3 if causal else 1)
    return pl.pallas_call(
        functools.partial(
            attend_back_kernel,
            heads=heads,
            causal=causal,
            blocks=blocks,
            key_blocks=key_blocks,
            per=per,
        ),
        grid_spec=pltpu.PrefetchScalarGridSpec(
            num_scalar_prefetch=1,
            grid=(repeat, key_blocks),
            in_specs=in_specs,
            out_specs=[
                pl.BlockSpec((rows, WIDE), lambda r, j, plan: (0, r)),
                pl.BlockSpec((BLOCK, WIDE), lambda r, j, plan: (turned(j, plan), r)),
                pl.BlockSpec((BLOCK, WIDE), lambda r, j, plan: (turned(j, plan), r)),
            ],
            scratch_shapes=[
                pltpu.VMEM((heads, rows, WIDE), LOW),
                pltpu.VMEM((heads, rows, WIDE), LOW),
                pltpu.VMEM((8, rows), F32),
                pltpu.VMEM((WIDE, rows), F32),
                pltpu.VMEM((BLOCK, WIDE), F32),
                pltpu.VMEM((BLOCK, WIDE), F32),
            ],
        ),
        out_shape=[
            jax.ShapeDtypeStruct((rows, WIDE * repeat), LOW),
            jax.ShapeDtypeStruct((keys, WIDE * repeat), LOW),
            jax.ShapeDtypeStruct((keys, WIDE * repeat), LOW),
        ],
        cost_estimate=pl.CostEstimate(
            flops=area * HEAD_DIM * 40, bytes_accessed=rows * 6000, transcendentals=area
        ),
        name="attend_self_back" if causal else "attend_cross_back",
    )(plan, *operands)


def norm_forward(values, gain, bias):
    average = jnp.mean(values, axis=-1, keepdims=True)
    centred = values - average
    scale = lax.rsqrt(jnp.mean(centred * centred, axis=-1, keepdims=True) + EPSILON)
    return (centred * scale * gain + bias).astype(LOW), (average, scale)


def norm_backward(values, kept, gain, grad):
    average, scale = kept
    unit = (values - average) * scale
    inner = grad * gain
    into = scale * (
        inner
        - jnp.mean(inner, axis=-1, keepdims=True)
        - unit * jnp.mean(inner * unit, axis=-1, keepdims=True)
    )
    return into, jnp.sum(grad * unit, axis=0), jnp.sum(grad, axis=0)


def pad_cols(piece):
    return jnp.pad(piece, ((0, 0), (0, WIDE - piece.shape[1])))


def pad_rows(piece):
    return jnp.pad(piece, ((0, WIDE - piece.shape[0]), (0, 0)))


def gelu_pair(inputs):
    root = 0.7978845608028654
    square = inputs * inputs
    bend = jnp.tanh(root * (inputs + 0.044715 * inputs * square))
    value = 0.5 * inputs * (1.0 + bend)
    slope = 0.5 * (1.0 + bend) + 0.5 * inputs * (1.0 - bend * bend) * root * (
        1.0 + 3.0 * 0.044715 * square
    )
    return value.astype(LOW), slope.astype(LOW)


def shards(
    tokens,
    context,
    segment_ids,
    frame_ids,
    context_lengths,
    cross_gain,
    cross_bias,
    cross_query,
    cross_key,
    cross_value,
    cross_out,
    attn_gain,
    attn_bias,
    attn_query,
    attn_key,
    attn_value,
    attn_out,
    mlp_gain,
    mlp_bias,
    mlp_up,
    mlp_down,
    out_grad,
):
    turn = lax.axis_index("tensor")
    rows = tokens.shape[0]
    group_rows = segment_ids.shape[0]
    pieces = group_rows // rows
    cols = cross_query.shape[1]
    heads = cols // HEAD_DIM
    own_context = context.shape[0]
    context_rows = own_context * pieces

    clips = jnp.arange(context_lengths.shape[0], dtype=jnp.int32)
    clip_ends = jnp.cumsum(context_lengths).astype(jnp.int32)
    clip_starts = clip_ends - context_lengths
    context_ids = jnp.arange(context_rows, dtype=jnp.int32)
    context_clip = jnp.sum((context_ids[:, None] >= clip_ends[None, :]).astype(jnp.int32), axis=1)
    own_segments = lax.dynamic_slice_in_dim(segment_ids, turn * rows, rows, 0)
    mark_lane = jnp.arange(128, dtype=jnp.int32)[None, :] - (cols - 128)

    def query_marks(ids):
        return (mark_lane == ids[:, None]).astype(LOW)

    def key_marks(ids):
        inside = (mark_lane >= 0) & (mark_lane < clips.shape[0])
        return jnp.where(inside & (mark_lane != ids[:, None]), FAR, 0.0).astype(LOW)

    def count(flags):
        return jnp.sum(flags.astype(jnp.int32), axis=1)

    seg_first, seg_last = segment_ids[::BLOCK], segment_ids[BLOCK - 1 :: BLOCK]
    self_low = count(segment_ids[None, :] < seg_first[:, None]) // BLOCK
    self_high = (count(segment_ids[None, :] <= seg_last[:, None]) - 1) // BLOCK + 1
    here = jnp.zeros((1,), jnp.int32) + turn
    still = jnp.zeros((1,), jnp.int32)
    self_plan = jnp.concatenate([here, self_low, self_low, self_low, self_high])
    self_marks = (query_marks(segment_ids), key_marks(segment_ids))
    own_first, own_last = own_segments[::BLOCK], own_segments[BLOCK - 1 :: BLOCK]

    def at_clip(table, ids):
        return jnp.sum(jnp.where(ids[:, None] == clips[None, :], table[None, :], 0), axis=1)

    cross_low = at_clip(clip_starts, own_first) // BLOCK
    cross_high = (at_clip(clip_ends, own_last) - 1) // BLOCK + 1
    key_first, key_last = context_clip[::BLOCK], context_clip[BLOCK - 1 :: BLOCK]
    back_low = count(own_segments[None, :] < key_first[:, None]) // BLOCK
    back_high = (count(own_segments[None, :] <= key_last[:, None]) + BLOCK - 1) // BLOCK
    cross_plan = jnp.concatenate([still, cross_low, cross_high, back_low, back_high])
    cross_marks = (query_marks(own_segments), key_marks(context_clip))

    context_pieces = gather_pieces(context)
    query_pieces = gather_pieces(cross_query)
    context_all = jnp.zeros((context_rows, context.shape[1]), LOW)
    for r in range(4):
        context_all = lax.dynamic_update_slice_in_dim(
            context_all, context_pieces[r], (turn ^ r) * own_context, 0
        )
    pair_weight = jnp.concatenate([cross_key, cross_value], axis=1)
    pair = dot(context_all, pair_weight, 1, 0).astype(LOW)
    pair_pieces = gather_pieces(pair)
    out_pieces = gather_pieces(cross_out)
    start = tokens.astype(F32)
    normed1, kept1 = norm_forward(start, cross_gain, cross_bias)
    query_weight = jnp.concatenate([pad_cols(p) for p in query_pieces], axis=1)
    query1 = dot(normed1, query_weight, 1, 0).astype(LOW)
    key1 = jnp.concatenate([pad_cols(p[:, :cols]) for p in pair_pieces], axis=1)
    value1 = jnp.concatenate([pad_cols(p[:, cols:]) for p in pair_pieces], axis=1)
    mixed1, stats1 = attend(
        cross_plan, (query1, key1, value1), (0, 0, 0), cross_marks, None, WIDE, heads, 4, 1
    )
    out_weight1 = jnp.concatenate([pad_rows(p) for p in out_pieces], axis=0)
    hidden1 = start + dot(mixed1, out_weight1, 1, 0)

    normed2, kept2 = norm_forward(hidden1, attn_gain, attn_bias)
    normed2_all = jnp.concatenate(gather_pieces(normed2), axis=0)
    self_weight = jnp.concatenate(
        [pad_cols(attn_query), pad_cols(attn_key), pad_cols(attn_value)], axis=1
    )
    triple = dot(normed2_all, self_weight, 1, 0).astype(LOW)
    per = rows // BLOCK
    mixed2, stats2 = attend(
        self_plan, (triple, triple, triple), (0, 1, 2), self_marks, frame_ids, cols, heads, 1, per
    )
    out2_pieces = gather_pieces(attn_out)
    out_weight2 = jnp.concatenate([pad_rows(p) for p in out2_pieces], axis=0)
    mixed2_own = jnp.concatenate(
        [
            pad_cols(p)
            for p in trade_pieces([mixed2[r * rows : (r + 1) * rows] for r in range(4)])
        ],
        axis=1,
    )
    hidden2 = hidden1 + dot(mixed2_own, out_weight2, 1, 0)

    up_pieces = gather_pieces(mlp_up)
    down_pieces = gather_pieces(mlp_down)
    normed3, kept3 = norm_forward(hidden2, mlp_gain, mlp_bias)
    final = hidden2
    normed3_grad = jnp.zeros((rows, tokens.shape[1]), F32)
    down_grads, up_grads = [], []
    for r in range(4):
        activated, slope = gelu_pair(dot(normed3, up_pieces[r], 1, 0))
        final = final + dot(activated, down_pieces[r], 1, 0)
        upper_grad = (dot(out_grad, down_pieces[r], 1, 1) * slope.astype(F32)).astype(LOW)
        down_grads.append(dot(activated, out_grad, 0, 0))
        up_grads.append(dot(normed3, upper_grad, 0, 0))
        normed3_grad = normed3_grad + dot(upper_grad, up_pieces[r], 1, 1)
    block_out = final.astype(LOW)
    mlp_down_grad = sum_over_groups(reduce_pieces(down_grads), 0)
    mlp_up_grad = sum_over_groups(reduce_pieces(up_grads), 1)
    into3, mlp_gain_part, mlp_bias_part = norm_backward(hidden2, kept3, mlp_gain, normed3_grad)
    grad2 = out_grad.astype(F32) + into3

    grad2_low = grad2.astype(LOW)
    mixed2_grad = dot(grad2_low, out_weight2, 1, 1).astype(LOW)
    out2_grads = dot(mixed2_own, grad2_low, 0, 0)
    traded = trade_pieces([mixed2_grad[:, r * WIDE : r * WIDE + cols] for r in range(4)])
    traded = jnp.concatenate([pad_cols(p) for p in traded], axis=0)
    query2_grad, key2_grad, value2_grad = attend_back(
        self_plan,
        (triple, triple, triple),
        (0, 1, 2),
        traded,
        mixed2,
        cols,
        stats2,
        self_marks,
        frame_ids,
        heads,
        1,
        per,
    )
    triple_grad = jnp.concatenate([query2_grad, key2_grad, value2_grad], axis=1)
    normed2_parts = [
        dot(triple_grad[r * rows : (r + 1) * rows], self_weight, 1, 1) for r in range(4)
    ]
    normed2_grad = reduce_pieces(normed2_parts)
    self_weight_grad = dot(normed2_all, triple_grad, 0, 0)
    attn_out_grad = sum_over_groups(
        reduce_pieces([out2_grads[r * WIDE : r * WIDE + cols] for r in range(4)]), 0
    )
    triple_weight_grad = sum_over_groups(
        jnp.concatenate(
            [self_weight_grad[:, s * WIDE : s * WIDE + cols] for s in range(3)], axis=1
        ),
        1,
    )
    into2, attn_gain_part, attn_bias_part = norm_backward(hidden1, kept2, attn_gain, normed2_grad)
    grad1 = grad2 + into2

    grad1_low = grad1.astype(LOW)
    mixed1_grad = dot(grad1_low, out_weight1, 1, 1).astype(LOW)
    out1_grads = dot(mixed1, grad1_low, 0, 0)
    query1_grad, key1_grad, value1_grad = attend_back(
        cross_plan,
        (query1, key1, value1),
        (0, 0, 0),
        mixed1_grad,
        mixed1,
        WIDE,
        stats1,
        cross_marks,
        None,
        heads,
        4,
        1,
    )
    pair_grad = reduce_pieces(
        [
            jnp.concatenate(
                [key1_grad[:, r * WIDE : r * WIDE + cols], value1_grad[:, r * WIDE : r * WIDE + cols]],
                axis=1,
            )
            for r in range(4)
        ]
    ).astype(LOW)
    query_weight_grads = dot(normed1, query1_grad, 0, 0)
    normed1_grad = dot(query1_grad, query_weight, 1, 1)
    cross_out_grad = sum_over_groups(
        reduce_pieces([out1_grads[r * WIDE : r * WIDE + cols] for r in range(4)]), 0
    )
    pair_weight_grad = sum_over_groups(dot(context_all, pair_grad, 0, 0), 1)
    cross_query_grad = sum_over_groups(
        reduce_pieces([query_weight_grads[:, r * WIDE : r * WIDE + cols] for r in range(4)]), 0
    )
    context_part = dot(pair_grad, pair_weight, 1, 1)
    context_grad = reduce_pieces(
        [
            lax.dynamic_slice_in_dim(context_part, (turn ^ r) * own_context, own_context, 0)
            for r in range(4)
        ]
    )
    into1, cross_gain_part, cross_bias_part = norm_backward(
        start, kept1, cross_gain, normed1_grad
    )
    tokens_grad = grad1 + into1

    small = sum_everywhere(
        jnp.stack(
            [
                cross_gain_part,
                cross_bias_part,
                attn_gain_part,
                attn_bias_part,
                mlp_gain_part,
                mlp_bias_part,
            ]
        )
    )
    return (
        block_out,
        tokens_grad,
        context_grad,
        small[0],
        small[1],
        cross_query_grad,
        pair_weight_grad[:, :cols],
        pair_weight_grad[:, cols:],
        cross_out_grad,
        small[2],
        small[3],
        triple_weight_grad[:, :cols],
        triple_weight_grad[:, cols : 2 * cols],
        triple_weight_grad[:, 2 * cols :],
        attn_out_grad,
        small[4],
        small[5],
        mlp_up_grad,
        mlp_down_grad,
    )


def solution(mesh):
    in_specs = (
        P(("dp", "tensor"), None),
        P(("dp", "tensor"), None),
        P("dp"),
        P("dp"),
        P("dp"),
        P(),
        P(),
        P(None, "tensor"),
        P(None, "tensor"),
        P(None, "tensor"),
        P("tensor", None),
        P(),
        P(),
        P(None, "tensor"),
        P(None, "tensor"),
        P(None, "tensor"),
        P("tensor", None),
        P(),
        P(),
        P(None, "tensor"),
        P("tensor", None),
        P(("dp", "tensor"), None),
    )
    out_specs = (
        P(("dp", "tensor"), None),
        P(("dp", "tensor"), None),
        P(("dp", "tensor"), None),
        P(),
        P(),
        P(None, "tensor"),
        P(None, "tensor"),
        P(None, "tensor"),
        P("tensor", None),
        P(),
        P(),
        P(None, "tensor"),
        P(None, "tensor"),
        P(None, "tensor"),
        P("tensor", None),
        P(),
        P(),
        P(None, "tensor"),
        P("tensor", None),
    )
    return jax.shard_map(shards, mesh=mesh, in_specs=in_specs, out_specs=out_specs, check_vma=False)
```

time: 1160 us -> 603 us (0.52)
  waiting for transfers between devices: 630 us -> 260 us
  matrix products: 245 us -> 81.2 us
  starting transfers between devices: 1.33 us -> 99.4 us
  Pallas kernels: 0 us -> 87.7 us
  other arithmetic: 106 us -> 41.7 us
  blocking collectives: 53.8 us -> 0 us
  local copies, waits for them, and re-layouts: 77.1 us -> 26.7 us
  loops' own time: 27.5 us -> 0 us
  between operations: 15.1 us -> 2.67 us
    psum x1 -> x0, waiting for transfers between devices: 265 us -> none  [shards(): lax.psum((cross_query_grad, cross_key_grad, cross_value_grad, cross_out_g...]
    ppermute x0 -> x101, waiting for transfers between devices: none -> 260 us  [swap(): return lax.ppermute(values, axis, [(i, i ^ bit) for i in range(size)])]
    reduce_scatter x7 -> x0, waiting for transfers between devices: 213 us -> none  [the longest x3 114 us: spread_rows(): lax.psum_scatter(jnp.dot(mixed_rows, weight, preferred_element_type=jnp.f...]
    dot_general x77 -> x42, matrix products: 245 us -> 81.2 us  [dot(): lax.dot_general(left, right, (((left_dim,), (right_dim,)), ((), ())), pre...]
    all_gather x6 -> x0, waiting for transfers between devices: 151 us -> none  [the longest x3 82.8 us: gather_grad(): lax.all_gather(gradient.astype(jnp.bfloat16), 'tensor', axis=0, tiled=True)]
    ppermute x0 -> x101, starting transfers between devices: none -> 99.4 us  [swap(): return lax.ppermute(values, axis, [(i, i ^ bit) for i in range(size)])]
    pallas_call x0 -> x4, Pallas kernels: none -> 87.7 us  [the longest x2 44.8 us: attend(): pl.pallas_call(functools.partial(attend_kernel, heads=heads, causal=causa...]
    reduce_sum x20 -> x9, other arithmetic: 51.4 us -> 5.72 us  [the longest x3 2.09 us: norm_forward(): jnp.mean(centred * centred, axis=-1, keepdims=True) + EPSILON]
  transfers between devices with their start and end apart: 14 -> 101, of which waited for: 13 -> 54; matrix products, arithmetic and copies ran while one was open for 5% -> 21% of each run, Pallas kernels for 0% -> 15%
where the time goes in v1:
time: 603 us; the launch traced here: 600 us
  waiting for transfers between devices  260 us (43%)
  starting transfers between devices  99.4 us (16%)
  Pallas kernels  87.7 us (15%)
  matrix products  81.2 us (13%)
  other arithmetic  41.7 us (7%)
  local copies, waits for them, and re-layouts  26.7 us (4%)
    ppermute x101, waiting for transfers between devices, swap(): return lax.ppermute(values, axis, [(i, i ^ bit) for i in range(size)])  260 us
    ppermute x101, starting transfers between devices, swap(): return lax.ppermute(values, axis, [(i, i ^ bit) for i in range(size)])  99.4 us
    dot_general x42, matrix products, dot(): lax.dot_general(left, right, (((left_dim,), (right_dim,)), ((), ())), pre...  81.2 us
    pallas_call x2, Pallas kernels, attend(): pl.pallas_call(functools.partial(attend_kernel, heads=heads, causal=causa...  44.8 us
    pallas_call x2, Pallas kernels, attend_back(): pl.pallas_call(functools.partial(attend_back_kernel, heads=heads, causal=...  42.8 us
  transfers between devices with their start and end apart: 101, of which 54 were waited for; matrix products, arithmetic and copies ran while one was open for 21% of the time, Pallas kernels for 15%

profile of v1, /device:TPU:0, one launch (start us, length us, event | category | flops | bytes accessed | tf_op | source)
XLA Modules:
  0.0 599.5 jit_solution(6213966405447570198)
XLA Ops:
  22.5 7.3 %collective-permute-done.7 = bf16[512,384]{1,0:T(8,128)(2,1)S(1)} collective-permute-done((bf16[512,384]{1,0:T(8,128)(2,1)S(1)}, bf16[512,384]{1,0:T(8,128)(2,1)S(1)}, u32[]{:S(2)}, u32[]{:S(2)}) %collective-permute-start.7) | collective-permute-done | bytes 393248 | tf_op jit(solution)/shard_map/ppermute | solution.py:27
  34.6 16.0 %attend_cross.1 = (bf16[512,1024]{1,0:T(8,128)(2,1)}, f32[32,512]{1,0:T(8,128)}) custom-call(s32[9]{0:T(128)} %concatenate.181.plan, bf16[512,1024]{1,0:T(8,128)(2,1)} %convolution_convert_fusion.15.q_ref, bf16[512,1024]{1,0:T(8,128)(2,1)} %get-tuple-element.238.k_ref, bf16[512,1024]{1,0:T(8,128)(2,1)} %get-tuple-element.237.v_ref, ...), custom_call_target="tpu_custom_call" | custom-call | flops 3221225472 | bytes 1536000 | tf_op jit(solution)/shard_map/attend_cross/pallas_call | solution.py:181
  55.6 11.8 %collective-permute-start.13 = (bf16[512,768]{1,0:T(8,128)(2,1)S(1)}, bf16[512,768]{1,0:T(8,128)(2,1)}, u32[]{:S(2)}, u32[]{:S(2)}) collective-permute-start(bf16[512,768]{1,0:T(8,128)(2,1)S(1)} %add_convert_fusion.11), channel_id=1, source_target_pairs={{0,2},{1,3},{2,0},{3,1},{4,6},{5,7},{6,4},{7,5},{8,10},{9,11},{10,... | collective-permute-start | bytes 2359304 | tf_op jit(solution)/shard_map/ppermute | solution.py:27
  72.0 13.9 %collective-permute-done.13 = bf16[512,768]{1,0:T(8,128)(2,1)} collective-permute-done((bf16[512,768]{1,0:T(8,128)(2,1)S(1)}, bf16[512,768]{1,0:T(8,128)(2,1)}, u32[]{:S(2)}, u32[]{:S(2)}) %collective-permute-start.13) | collective-permute-done | bytes 786464 | tf_op jit(solution)/shard_map/ppermute | solution.py:27
  94.3 6.2 %convolution_convert_fusion.q_ref.k_ref.v_ref = bf16[2048,768]{1,0:T(8,128)(2,1)} fusion(bf16[512,768]{1,0:T(8,128)(2,1)S(1)} %collective-permute-done.14, bf16[512,768]{1,0:T(8,128)(2,1)} %collective-permute-done.13, bf16[512,768]{1,0:T(8,128)(2,1)S(1)} %collective-permute-done.12, bf16[512,768]{1,0:T(8,128)(2,1)S(1)} %add_convert_fusion.11, ...), kind=kOutput, calls=%fused_computation.10 | convolution fusion | flops 2438332416 | bytes 7176192 | tf_op jit(solution)/shard_map/dot_general | solution.py:20
  100.6 28.8 %attend_self.1 = (bf16[2048,192]{1,0:T(8,128)(2,1)}, f32[8,2048]{1,0:T(8,128)}) custom-call(s32[33]{0:T(128)} %concatenate.187.plan, bf16[2048,768]{1,0:T(8,128)(2,1)} %convolution_convert_fusion.q_ref.k_ref.v_ref, bf16[2048,768]{1,0:T(8,128)(2,1)} %convolution_convert_fusion.q_ref.k_ref.v_ref, bf16[2048,768]{1,0:T(8,128)(2,1)} %convolution_convert_fusion.q_ref.k_ref.v_ref, ...), custom_call_target="tpu_custom_call" | custom-call | flops 4294967296 | bytes 6144000 | tf_op jit(solution)/shard_map/attend_self/pallas_call | solution.py:181
  133.1 9.0 %collective-permute-done.23 = bf16[768,768]{1,0:T(8,128)(2,1)} collective-permute-done((bf16[768,768]{1,0:T(8,128)(2,1)}, bf16[768,768]{1,0:T(8,128)(2,1)}, u32[]{:S(2)}, u32[]{:S(2)}) %collective-permute-start.23) | collective-permute-done | bytes 1179680 | tf_op jit(solution)/shard_map/ppermute | solution.py:27
  208.6 25.3 %attend_self_back.1 = (bf16[2048,256]{1,0:T(8,128)(2,1)}, bf16[2048,256]{1,0:T(8,128)(2,1)}, bf16[2048,256]{1,0:T(8,128)(2,1)}) custom-call(s32[33]{0:T(128)} %concatenate.187.plan, bf16[2048,768]{1,0:T(8,128)(2,1)} %convolution_convert_fusion.q_ref.k_ref.v_ref, bf16[2048,768]{1,0:T(8,128)(2,1)} %convolution_convert_fusion.q_ref.k_ref.v_ref, ...), custom_call_target="tpu_custom_call" | custom-call | flops 10737418240 | bytes 12288000 | tf_op jit(solution)/shard_map/attend_self_back/pallas_call | solution.py:333
  246.9 6.4 %collective-permute-done.76 = bf16[192,768]{1,0:T(8,128)(2,1)S(1)} collective-permute-done((bf16[192,768]{1,0:T(8,128)(2,1)S(1)}, bf16[192,768]{1,0:T(8,128)(2,1)S(1)}, u32[]{:S(2)}, u32[]{:S(2)}) %collective-permute-start.76) | collective-permute-done | bytes 294944 | tf_op jit(solution)/shard_map/ppermute | solution.py:27
  264.5 10.9 %collective-permute-start.79 = (bf16[24,768]{1,0:T(8,128)(2,1)S(1)}, bf16[24,768]{1,0:T(8,128)(2,1)S(1)}, u32[]{:S(2)}, u32[]{:S(2)}) collective-permute-start(bf16[24,768]{1,0:T(8,128)(2,1)S(1)} %constant_dynamic-slice_fusion.6), channel_id=1, source_target_pairs={{0,16},{4,20},{8,24},{12,28},{16,0},{20,4},{24,8},{28,12},{1,17},{... | collective-permute-start | bytes 110600 | tf_op jit(solution)/shard_map/ppermute | solution.py:27
  280.4 12.3 %collective-permute-done.69 = bf16[192,576]{0,1:T(8,128)(2,1)S(1)} collective-permute-done((bf16[192,576]{0,1:T(8,128)(2,1)S(1)}, bf16[192,576]{0,1:T(8,128)(2,1)S(1)}, u32[]{:S(2)}, u32[]{:S(2)}) %collective-permute-start.69) | collective-permute-done | bytes 221216 | tf_op jit(solution)/shard_map/ppermute | solution.py:27
  292.9 4.9 collective-permute-done.80
  319.5 7.0 %collective-permute-done.72 = bf16[192,576]{0,1:T(8,128)(2,1)S(1)} collective-permute-done((bf16[192,576]{0,1:T(8,128)(2,1)S(1)}, bf16[192,576]{0,1:T(8,128)(2,1)S(1)}, u32[]{:S(2)}, u32[]{:S(2)}) %collective-permute-start.72) | collective-permute-done | bytes 221216 | tf_op jit(solution)/shard_map/ppermute | solution.py:27
  337.1 9.9 %collective-permute-done.32 = bf16[512,768]{1,0:T(8,128)(2,1)S(1)} collective-permute-done((bf16[512,768]{1,0:T(8,128)(2,1)S(1)}, bf16[512,768]{1,0:T(8,128)(2,1)S(1)}, u32[]{:S(2)}, u32[]{:S(2)}) %collective-permute-start.32) | collective-permute-done | bytes 786464 | tf_op jit(solution)/shard_map/ppermute | solution.py:27
  353.3 17.5 %attend_cross_back.1 = (bf16[512,1024]{1,0:T(8,128)(2,1)}, bf16[512,1024]{1,0:T(8,128)(2,1)}, bf16[512,1024]{1,0:T(8,128)(2,1)}) custom-call(s32[9]{0:T(128)} %concatenate.181.plan, bf16[512,1024]{1,0:T(8,128)(2,1)} %convolution_convert_fusion.15.q_ref, bf16[512,1024]{1,0:T(8,128)(2,1)} %get-tuple-element.238.k_ref, ...), custom_call_target="tpu_custom_call" | custom-call | flops 8053063680 | bytes 3072000 | tf_op jit(solution)/shard_map/attend_cross_back/pallas_call | solution.py:333
  390.0 6.0 %collective-permute-start.40 = (f32[6,768]{1,0:T(8,128)S(1)}, f32[6,768]{1,0:T(8,128)S(1)}, u32[]{:S(2)}, u32[]{:S(2)}) collective-permute-start(f32[6,768]{1,0:T(8,128)S(1)} %add.567), channel_id=1, source_target_pairs={{0,2},{1,3},{2,0},{3,1},{4,6},{5,7},{6,4},{7,5},{8,10},{9,11},{10,... | collective-permute-start | bytes 55304 | tf_op jit(solution)/shard_map/ppermute | solution.py:27
  415.6 6.4 %collective-permute-done.61 = bf16[192,768]{1,0:T(8,128)(2,1)S(1)} collective-permute-done((bf16[192,768]{1,0:T(8,128)(2,1)S(1)}, bf16[192,768]{1,0:T(8,128)(2,1)S(1)}, u32[]{:S(2)}, u32[]{:S(2)}) %collective-permute-start.61) | collective-permute-done | bytes 294944 | tf_op jit(solution)/shard_map/ppermute | solution.py:27
  424.1 31.3 %collective-permute-done.46 = bf16[768,192]{1,0:T(8,128)(2,1)S(1)} collective-permute-done((bf16[768,192]{1,0:T(8,128)(2,1)S(1)}, bf16[768,192]{1,0:T(8,128)(2,1)S(1)}, u32[]{:S(2)}, u32[]{:S(2)}) %collective-permute-start.46) | collective-permute-done | bytes 294944 | tf_op jit(solution)/shard_map/ppermute | solution.py:27
  471.9 7.6 %collective-permute-done.48 = bf16[192,192]{1,0:T(8,128)(2,1)S(1)} collective-permute-done((bf16[192,192]{1,0:T(8,128)(2,1)S(1)}, bf16[192,192]{1,0:T(8,128)(2,1)S(1)}, u32[]{:S(2)}, u32[]{:S(2)}) %collective-permute-start.48) | collective-permute-done | bytes 73760 | tf_op jit(solution)/shard_map/ppermute | solution.py:27
  490.9 5.3 collective-permute-done.50
  512.5 6.0 %collective-permute-done.53 = bf16[384,384]{1,0:T(8,128)(2,1)S(1)} collective-permute-done((bf16[384,384]{1,0:T(8,128)(2,1)S(1)}, bf16[384,384]{1,0:T(8,128)(2,1)S(1)}, u32[]{:S(2)}, u32[]{:S(2)}) %collective-permute-start.53) | collective-permute-done | bytes 294944 | tf_op jit(solution)/shard_map/ppermute | solution.py:27
  522.4 7.3 %collective-permute-done.54 = bf16[192,384]{1,0:T(8,128)(2,1)S(1)} collective-permute-done((bf16[192,384]{1,0:T(8,128)(2,1)S(1)}, bf16[192,384]{1,0:T(8,128)(2,1)S(1)}, u32[]{:S(2)}, u32[]{:S(2)}) %collective-permute-start.54) | collective-permute-done | bytes 147488 | tf_op jit(solution)/shard_map/ppermute | solution.py:27
  554.4 9.0 %collective-permute-done.97 = bf16[96,768]{1,0:T(8,128)(2,1)S(1)} collective-permute-done((bf16[96,768]{1,0:T(8,128)(2,1)S(1)}, bf16[96,768]{1,0:T(8,128)(2,1)S(1)}, u32[]{:S(2)}, u32[]{:S(2)}) %collective-permute-start.97) | collective-permute-done | bytes 147488 | tf_op jit(solution)/shard_map/ppermute | solution.py:27
  576.3 5.7 collective-permute-done.90
  (534 shorter events, 324.8 us)
Async XLA Ops:
  13.5 37.2 %collective-permute-start.9 = (bf16[192,768]{1,0:T(8,128)(2,1)}, bf16[192,768]{1,0:T(8,128)(2,1)}, u32[]{:S(2)}, u32[]{:S(2)}) collective-permute-start(bf16[192,768]{1,0:T(8,128)(2,1)} %param.32), channel_id=1, source_target_pairs={{0,1},{1,0},{2,3},{3,2},{4,5},{5,4},{6,7},{7,6},{8,9},{9,8},{10,11... | collective-permute-start | bytes 884744 | tf_op jit(solution)/shard_map/ppermute | solution.py:27
  21.8 28.9 %collective-permute-start.11 = (bf16[192,768]{1,0:T(8,128)(2,1)}, bf16[192,768]{1,0:T(8,128)(2,1)S(1)}, u32[]{:S(2)}, u32[]{:S(2)}) collective-permute-start(bf16[192,768]{1,0:T(8,128)(2,1)} %collective-permute-done.10), channel_id=1, source_target_pairs={{0,1},{1,0},{2,3},{3,2},{4,5},{5,4},{6,7},{7,6},{8,9},{9,8},{10,11... | collective-permute-start | bytes 884744 | tf_op jit(solution)/shard_map/ppermute | solution.py:27
  55.6 30.4 %collective-permute-start.13 = (bf16[512,768]{1,0:T(8,128)(2,1)S(1)}, bf16[512,768]{1,0:T(8,128)(2,1)}, u32[]{:S(2)}, u32[]{:S(2)}) collective-permute-start(bf16[512,768]{1,0:T(8,128)(2,1)S(1)} %add_convert_fusion.11), channel_id=1, source_target_pairs={{0,2},{1,3},{2,0},{3,1},{4,6},{5,7},{6,4},{7,5},{8,10},{9,11},{10,... | collective-permute-start | bytes 2359304 | tf_op jit(solution)/shard_map/ppermute | solution.py:27
  67.5 63.3 %collective-permute-start.18 = (bf16[192,768]{1,0:T(8,128)(2,1)}, bf16[192,768]{1,0:T(8,128)(2,1)}, u32[]{:S(2)}, u32[]{:S(2)}) collective-permute-start(bf16[192,768]{1,0:T(8,128)(2,1)} %param.38), channel_id=1, source_target_pairs={{0,1},{1,0},{2,3},{3,2},{4,5},{5,4},{6,7},{7,6},{8,9},{9,8},{10,11... | collective-permute-start | bytes 884744 | tf_op jit(solution)/shard_map/ppermute | solution.py:27
  67.5 65.1 %collective-permute-start.24 = (bf16[768,768]{1,0:T(8,128)(2,1)}, bf16[768,768]{1,0:T(8,128)(2,1)}, u32[]{:S(2)}, u32[]{:S(2)}) collective-permute-start(bf16[768,768]{1,0:T(8,128)(2,1)} %param.42), channel_id=1, source_target_pairs={{0,2},{1,3},{2,0},{3,1},{4,6},{5,7},{6,4},{7,5},{8,10},{9,11},{10,... | collective-permute-start | bytes 3538952 | tf_op jit(solution)/shard_map/ppermute | solution.py:27
  92.3 49.8 %collective-permute-start.23 = (bf16[768,768]{1,0:T(8,128)(2,1)}, bf16[768,768]{1,0:T(8,128)(2,1)}, u32[]{:S(2)}, u32[]{:S(2)}) collective-permute-start(bf16[768,768]{1,0:T(8,128)(2,1)} %param.41), channel_id=1, source_target_pairs={{0,2},{1,3},{2,0},{3,1},{4,6},{5,7},{6,4},{7,5},{8,10},{9,11},{10,... | collective-permute-start | bytes 3538952 | tf_op jit(solution)/shard_map/ppermute | solution.py:27
  94.3 38.3 %collective-permute-start.20 = (bf16[192,768]{1,0:T(8,128)(2,1)}, bf16[192,768]{1,0:T(8,128)(2,1)}, u32[]{:S(2)}, u32[]{:S(2)}) collective-permute-start(bf16[192,768]{1,0:T(8,128)(2,1)} %collective-permute-done.19), channel_id=1, source_target_pairs={{0,1},{1,0},{2,3},{3,2},{4,5},{5,4},{6,7},{7,6},{8,9},{9,8},{10,11... | collective-permute-start | bytes 884744 | tf_op jit(solution)/shard_map/ppermute | solution.py:27
  145.1 36.4 %collective-permute-start.26 = (bf16[768,768]{1,0:T(8,128)(2,1)}, bf16[768,768]{1,0:T(8,128)(2,1)S(1)}, u32[]{:S(2)}, u32[]{:S(2)}) collective-permute-start(bf16[768,768]{1,0:T(8,128)(2,1)} %collective-permute-done.24), channel_id=1, source_target_pairs={{0,1},{1,0},{2,3},{3,2},{4,5},{5,4},{6,7},{7,6},{8,9},{9,8},{10,11... | collective-permute-start | bytes 3538952 | tf_op jit(solution)/shard_map/ppermute | solution.py:27
  198.1 45.2 %collective-permute-start.75 = (bf16[192,768]{1,0:T(8,128)(2,1)S(1)}, bf16[192,768]{1,0:T(8,128)(2,1)}, u32[]{:S(2)}, u32[]{:S(2)}) collective-permute-start(bf16[192,768]{1,0:T(8,128)(2,1)S(1)} %get-tuple-element.94), channel_id=1, source_target_pairs={{0,1},{1,0},{2,3},{3,2},{4,5},{5,4},{6,7},{7,6},{8,9},{9,8},{10,11... | collective-permute-start | bytes 884744 | tf_op jit(solution)/shard_map/ppermute | solution.py:27
  198.7 48.1 %collective-permute-start.74 = (bf16[192,768]{1,0:T(8,128)(2,1)S(1)}, bf16[192,768]{1,0:T(8,128)(2,1)}, u32[]{:S(2)}, u32[]{:S(2)}) collective-permute-start(bf16[192,768]{1,0:T(8,128)(2,1)S(1)} %get-tuple-element.92), channel_id=1, source_target_pairs={{0,1},{1,0},{2,3},{3,2},{4,5},{5,4},{6,7},{7,6},{8,9},{9,8},{10,11... | collective-permute-start | bytes 884744 | tf_op jit(solution)/shard_map/ppermute | solution.py:27
  204.5 122.7 %collective-permute-start.84 = (bf16[768,768]{1,0:T(8,128)(2,1)}, bf16[768,768]{1,0:T(8,128)(2,1)}, u32[]{:S(2)}, u32[]{:S(2)}) collective-permute-start(bf16[768,768]{1,0:T(8,128)(2,1)} %convolution_convert_fusion.8), channel_id=1, source_target_pairs={{0,1},{1,0},{2,3},{3,2},{4,5},{5,4},{6,7},{7,6},{8,9},{9,8},{10,11... | collective-permute-start | bytes 3538952 | tf_op jit(solution)/shard_map/ppermute | solution.py:27
  206.9 248.7 %collective-permute-start.83 = (bf16[768,768]{1,0:T(8,128)(2,1)}, bf16[768,768]{1,0:T(8,128)(2,1)}, u32[]{:S(2)}, u32[]{:S(2)}) collective-permute-start(bf16[768,768]{1,0:T(8,128)(2,1)} %convolution_convert_fusion.10), channel_id=1, source_target_pairs={{0,1},{1,0},{2,3},{3,2},{4,5},{5,4},{6,7},{7,6},{8,9},{9,8},{10,11... | collective-permute-start | bytes 3538952 | tf_op jit(solution)/shard_map/ppermute | solution.py:27
  206.9 123.5 %collective-permute-start.93 = (bf16[768,768]{1,0:T(8,128)(2,1)}, bf16[768,768]{1,0:T(8,128)(2,1)}, u32[]{:S(2)}, u32[]{:S(2)}) collective-permute-start(bf16[768,768]{1,0:T(8,128)(2,1)} %convolution_convert_fusion.4), channel_id=1, source_target_pairs={{0,1},{1,0},{2,3},{3,2},{4,5},{5,4},{6,7},{7,6},{8,9},{9,8},{10,11... | collective-permute-start | bytes 3538952 | tf_op jit(solution)/shard_map/ppermute | solution.py:27
  259.7 55.8 %collective-permute-start.31 = (bf16[512,768]{1,0:T(8,128)(2,1)S(1)}, bf16[512,768]{1,0:T(8,128)(2,1)S(1)}, u32[]{:S(2)}, u32[]{:S(2)}) collective-permute-start(bf16[512,768]{1,0:T(8,128)(2,1)S(1)} %convolution_convert_fusion.16), channel_id=1, source_target_pairs={{0,1},{1,0},{2,3},{3,2},{4,5},{5,4},{6,7},{7,6},{8,9},{9,8},{10,11... | collective-permute-start | bytes 2359304 | tf_op jit(solution)/shard_map/ppermute | solution.py:27
  330.4 127.0 %collective-permute-start.85 = (bf16[768,768]{1,0:T(8,128)(2,1)}, bf16[768,768]{1,0:T(8,128)(2,1)}, u32[]{:S(2)}, u32[]{:S(2)}) collective-permute-start(bf16[768,768]{1,0:T(8,128)(2,1)} %add_convert_fusion.3), channel_id=1, source_target_pairs={{0,2},{1,3},{2,0},{3,1},{4,6},{5,7},{6,4},{7,5},{8,10},{9,11},{10,... | collective-permute-start | bytes 3538952 | tf_op jit(solution)/shard_map/ppermute | solution.py:27
  414.4 45.2 %collective-permute-start.92 = (bf16[768,768]{1,0:T(8,128)(2,1)S(1)}, bf16[768,768]{1,0:T(8,128)(2,1)S(1)}, u32[]{:S(2)}, u32[]{:S(2)}) collective-permute-start(bf16[768,768]{1,0:T(8,128)(2,1)S(1)} %copy-done.53), channel_id=1, source_target_pairs={{0,1},{1,0},{2,3},{3,2},{4,5},{5,4},{6,7},{7,6},{8,9},{9,8},{10,11... | collective-permute-start | bytes 3538952 | tf_op jit(solution)/shard_map/ppermute | solution.py:27
  414.5 47.2 %collective-permute-start.94 = (bf16[768,768]{1,0:T(8,128)(2,1)S(1)}, bf16[768,768]{1,0:T(8,128)(2,1)S(1)}, u32[]{:S(2)}, u32[]{:S(2)}) collective-permute-start(bf16[768,768]{1,0:T(8,128)(2,1)S(1)} %add_convert_fusion.1), channel_id=1, source_target_pairs={{0,2},{1,3},{2,0},{3,1},{4,6},{5,7},{6,4},{7,5},{8,10},{9,11},{10,... | collective-permute-start | bytes 3538952 | tf_op jit(solution)/shard_map/ppermute | solution.py:27
  422.0 33.4 %collective-permute-start.46 = (bf16[768,192]{1,0:T(8,128)(2,1)S(1)}, bf16[768,192]{1,0:T(8,128)(2,1)S(1)}, u32[]{:S(2)}, u32[]{:S(2)}) collective-permute-start(bf16[768,192]{1,0:T(8,128)(2,1)S(1)} %add_convert_fusion.16), channel_id=1, source_target_pairs={{0,2},{1,3},{2,0},{3,1},{4,6},{5,7},{6,4},{7,5},{8,10},{9,11},{10,... | collective-permute-start | bytes 884744 | tf_op jit(solution)/shard_map/ppermute | solution.py:27
  461.7 59.0 %collective-permute-start.86 = (bf16[384,768]{1,0:T(8,128)(2,1)S(1)}, bf16[384,768]{1,0:T(8,128)(2,1)S(1)}, u32[]{:S(2)}, u32[]{:S(2)}) collective-permute-start(bf16[384,768]{1,0:T(8,128)(2,1)S(1)} %constant_dynamic-slice_fusion.5), channel_id=1, source_target_pairs={{0,8},{4,12},{8,0},{12,4},{16,24},{20,28},{24,16},{28,20},{1,9},{5... | collective-permute-start | bytes 1769480 | tf_op jit(solution)/shard_map/ppermute | solution.py:27
  465.1 64.7 %collective-permute-start.95 = (bf16[384,768]{1,0:T(8,128)(2,1)S(1)}, bf16[384,768]{1,0:T(8,128)(2,1)S(1)}, u32[]{:S(2)}, u32[]{:S(2)}) collective-permute-start(bf16[384,768]{1,0:T(8,128)(2,1)S(1)} %constant_dynamic-slice_fusion.2), channel_id=1, source_target_pairs={{0,4},{4,0},{8,12},{12,8},{16,20},{20,16},{24,28},{28,24},{1,5},{5... | collective-permute-start | bytes 1769480 | tf_op jit(solution)/shard_map/ppermute | solution.py:27
  471.1 39.3 %collective-permute-start.37 = (bf16[128,768]{1,0:T(8,128)(2,1)S(1)}, bf16[128,768]{1,0:T(8,128)(2,1)S(1)}, u32[]{:S(2)}, u32[]{:S(2)}) collective-permute-start(bf16[128,768]{1,0:T(8,128)(2,1)S(1)} %get-tuple-element.82), channel_id=1, source_target_pairs={{0,1},{1,0},{2,3},{3,2},{4,5},{5,4},{6,7},{7,6},{8,9},{9,8},{10,11... | collective-permute-start | bytes 589832 | tf_op jit(solution)/shard_map/ppermute | solution.py:27
  479.5 102.8 %collective-permute-start.36 = (bf16[128,768]{1,0:T(8,128)(2,1)S(1)}, bf16[128,768]{1,0:T(8,128)(2,1)}, u32[]{:S(2)}, u32[]{:S(2)}) collective-permute-start(bf16[128,768]{1,0:T(8,128)(2,1)S(1)} %get-tuple-element.80), channel_id=1, source_target_pairs={{0,1},{1,0},{2,3},{3,2},{4,5},{5,4},{6,7},{7,6},{8,9},{9,8},{10,11... | collective-permute-start | bytes 589832 | tf_op jit(solution)/shard_map/ppermute | solution.py:27
  518.5 50.1 %collective-permute-start.67 = (bf16[96,768]{1,0:T(8,128)(2,1)S(1)}, bf16[96,768]{1,0:T(8,128)(2,1)S(1)}, u32[]{:S(2)}, u32[]{:S(2)}) collective-permute-start(bf16[96,768]{1,0:T(8,128)(2,1)S(1)} %maximum_select_fusion.16), channel_id=1, source_target_pairs={{0,4},{4,0},{8,12},{12,8},{16,20},{20,16},{24,28},{28,24},{1,5},{5... | collective-permute-start | bytes 442376 | tf_op jit(solution)/shard_map/ppermute | solution.py:27
  520.3 62.0 %collective-permute-start.38 = (bf16[128,768]{1,0:T(8,128)(2,1)S(1)}, bf16[128,768]{1,0:T(8,128)(2,1)}, u32[]{:S(2)}, u32[]{:S(2)}) collective-permute-start(bf16[128,768]{1,0:T(8,128)(2,1)S(1)} %add_convert_fusion.28), channel_id=1, source_target_pairs={{0,2},{1,3},{2,0},{3,1},{4,6},{5,7},{6,4},{7,5},{8,10},{9,11},{10,... | collective-permute-start | bytes 589832 | tf_op jit(solution)/shard_map/ppermute | solution.py:27
  (144 other events, 1273.0 us)
